TPU v7x, 512 devices: a whole 4x8x8 slice. The times are simulated.
512 devices in a mesh: cells: 32 (over y, x), genes: 16 (over z, core).
Axes of the slice: x: 4, y: 8, z: 8, core: 2. Of those that a mesh axis runs over, the one named last changes fastest.
Arguments:
- counts: int32 [32768, 4096], P('cells', 'genes'), may hold values from 0 to 128, as said below
- batch: int32 [32768, 1], P(('cells', 'genes')), may hold values from 0 to 63
- seeds: int32 [32768, 1], P(('cells', 'genes')), may hold values from 0 to 1023
- loadings: bfloat16 [4096, 256], P('genes'), may hold values from -0.09375 to 0.09375
Outputs:
- embedding: float32 [32768, 256], P(('cells', 'genes'))
- assign: float32 [32768, 1024], P(('cells', 'genes'))
- centroids: bfloat16 [1024, 256], replicated
Inputs may be any that keep to these rules, and one draw needn't show every extreme that they name: counts[i, g] >= 1 wherever g mod 64 equals i mod 64. `batch`: every label occurs. `seeds`: every cluster is the seed of some cell.
All inputs are finite; a program needn't handle non-finite values.
Results may differ from a plain program's by a relative error of at most 0.012.
The roundings to bfloat16 on the way count: a program that leaves them out, or rounds other values in their place, can miss the bound.
Values may be sent and summed in bfloat16 or wider, within the bound.
No kernel may reach another device: no remote copies, remote signals or barrier semaphores. Data moves between devices by JAX's collectives and lax.ppermute only.
A program may use at most 64 MiB of HBM per device.

v0:
```python
import jax
import jax.numpy as jnp
from jax import lax
from jax.sharding import PartitionSpec as P

K = 1024
B = 64
ITERS = 2
X_SIZE = 4
Y_AXIS = "y"
X_AXIS = "x"
CELL_AXIS = (Y_AXIS, X_AXIS)
Z_AXIS = "z"
CORE_AXIS = "core"
GENE_AXIS = (Z_AXIS, CORE_AXIS)
epsilon = 1e-06
cluster_spread = 0.1
f32 = jnp.float32
bf16 = jnp.bfloat16
trailing = (((1,), (1,)), ((), ()))
together = lax.optimization_barrier


def exchange(blocks, axis):
    return lax.all_to_all(blocks, axis, 0, 0, tiled=False)


def share(block, axis):
    return exchange(jnp.broadcast_to(block[None], (lax.axis_size(axis),) + block.shape), axis)


def gather(block, axis):
    return lax.all_gather(block, axis, tiled=True)


def dot(left, right):
    return jnp.dot(left, right, preferred_element_type=f32)


def dot_rows(left, right):
    return lax.dot_general(left, right, trailing, preferred_element_type=f32)


def hot_columns(labels, count):
    return (labels[None, :] == jnp.arange(count, dtype=f32)[:, None]).astype(bf16)


def halves(value):
    high = value.astype(bf16)
    return (high, (value - high.astype(f32)).astype(bf16))


def unit(rows):
    scaled = rows * lax.rsqrt(jnp.sum(rows * rows, axis=1, keepdims=True) + epsilon)
    return scaled.astype(bf16)


def penalty_halves(observed, batch_total, total_cells):
    mass = jnp.sum(observed, axis=1, keepdims=True)
    ratio = (mass * batch_total / total_cells + 1.0) / (observed + 1.0)
    return jnp.concatenate(halves(ratio * ratio), axis=1)


def added(blocks):
    total = blocks[0].astype(f32)
    for at in range(1, blocks.shape[0]):
        total = total + blocks[at].astype(f32)
    return total


def folded(observed):
    half = observed.shape[0] // 2
    return jnp.concatenate([observed[:half], observed[half:]], axis=1).astype(bf16)


def everywhere(sums, fold):
    half, lanes = (sums.shape[0] // 2, sums.shape[1] // 2)
    sums = sums.astype(bf16)
    block = jnp.concatenate([sums[:, :lanes], sums[:, lanes:], fold], axis=0)
    for axis in (Y_AXIS, X_AXIS):
        block = added(share(block.astype(bf16), axis))
    sums = jnp.concatenate([block[: 2 * half], block[2 * half : 4 * half]], axis=1)
    observed = jnp.concatenate([block[4 * half :, :B], block[4 * half :, B:]], axis=0)
    return (sums, observed)


def weigh(similarity, lookup):
    distance = 2.0 - 2.0 * similarity
    return jnp.exp(-distance / cluster_spread) * lookup


def per_device(counts, batch, seeds, loadings):
    n_cells, n_genes = (lax.axis_size(CELL_AXIS), lax.axis_size(GENE_AXIS))
    n_z, n_core = (lax.axis_size(Z_AXIS), lax.axis_size(CORE_AXIS))
    group, own = (counts.shape[0], batch.shape[0])
    total_cells = group * n_cells
    width = loadings.shape[1]
    mine = K // n_genes
    values = counts.astype(f32)
    shares = dot_rows(jnp.ones((8, counts.shape[1]), bf16), counts.astype(bf16))
    packet = jnp.concatenate([shares[0], batch[:, 0].astype(f32), seeds[:, 0].astype(f32)])
    own_hot = (batch == jnp.arange(B, dtype=jnp.int32)[None, :]).astype(bf16)
    own_twice = jnp.concatenate([own_hot, own_hot], axis=1)
    first = (lax.axis_index(GENE_AXIS) * mine).astype(f32)
    even = lax.axis_index(CORE_AXIS) == 0
    packet, own_twice, first, even = together((packet, own_twice, first, even))
    packets = share(packet, GENE_AXIS)
    depth_total = jnp.sum(packets[:, :group], axis=0)
    labels = packets[:, group:].reshape(n_z, n_core, 2, own).transpose(2, 1, 0, 3)
    group_batch = labels[0].reshape(group)
    group_seeds = labels[1].reshape(group)
    logged = jnp.log1p(10000.0 * values / depth_total[:, None]).astype(bf16)
    partial = dot(logged, loadings)
    batch_hot = hot_columns(group_batch, B)
    batch_twice = jnp.concatenate([batch_hot, batch_hot], axis=0)
    assign = hot_columns(group_seeds - first, mine)
    first_fold = folded(dot_rows(assign, batch_hot))
    group_labels = dot_rows(jnp.ones((8, group), bf16), batch_hot)[0]
    packet = jnp.concatenate([jnp.sum(partial, axis=0), group_labels])
    packet, batch_hot, batch_twice, assign, first_fold = together(
        (packet, batch_hot, batch_twice, assign, first_fold)
    )
    arrived = jnp.sum(share(packet, CELL_AXIS), axis=0)
    center = arrived[:width] / total_cells
    batch_total = arrived[width:][None]
    centred = (partial - center[None]).reshape(n_z, n_core, own, width)
    kept = jnp.where(even, centred[:, 0], centred[:, 1])
    given = jnp.where(even, centred[:, 1], centred[:, 0]).astype(bf16)
    given, kept, batch_total = together((given, kept, batch_total))
    taken = lax.ppermute(given, CORE_AXIS, [(0, 1), (1, 0)])
    pairs = (kept + taken.astype(f32)).astype(bf16)
    embedding = jnp.sum(exchange(pairs, Z_AXIS).astype(f32), axis=0)
    own_rows = unit(embedding)
    unit_rows = gather(share(own_rows, Z_AXIS).reshape(n_z * own, width), CORE_AXIS)
    for iteration in range(ITERS):
        if iteration == 0:
            sums, fold = (dot(assign, unit_rows), first_fold)
        else:
            weights = weigh(dot_rows(rows[:, :width], unit_rows), dot(rows[:, width:], batch_twice))
            norm = jnp.sum(share(jnp.sum(weights, axis=0), GENE_AXIS), axis=0)
            rounded = (weights / norm[None, :]).astype(bf16)
            sums, fold = (dot(rounded, unit_rows), folded(dot_rows(rounded, batch_hot)))
        sums, observed = everywhere(sums, fold)
        penalty = penalty_halves(observed, batch_total, total_cells)
        rows = jnp.concatenate([unit(sums), penalty], axis=1)
    rows = gather(rows, GENE_AXIS)
    weights = weigh(dot_rows(own_rows, rows[:, :width]), dot_rows(own_twice, rows[:, width:]))
    assign = weights / jnp.sum(weights, axis=1, keepdims=True)
    return (embedding, assign, rows[:, :width])


def solution(mesh):
    cells, genes = mesh.devices.shape
    mesh = jax.sharding.Mesh(
        mesh.devices.reshape(cells // X_SIZE, X_SIZE, genes // 2, 2),
        (Y_AXIS, X_AXIS, Z_AXIS, CORE_AXIS),
    )
    owners = P((Y_AXIS, X_AXIS, Z_AXIS, CORE_AXIS), None)
    placed = (P(CELL_AXIS, GENE_AXIS), owners, owners, P(GENE_AXIS, None))
    return jax.shard_map(
        per_device, mesh=mesh, in_specs=placed, out_specs=(owners, owners, P()), check_vma=False
    )
```

profile of v0, /device:TPU:1, one launch (start us, length us, event | category | flops | bytes accessed | tf_op | source)
XLA Modules:
  0.0 160.9 jit_solution(14211592122687259710)
XLA Ops:
  0.7 1.5 fusion.9
  2.5 19.7 %all_to_all.51 = f32[16,1,1152]{2,1,0:T(1,128)S(1)} all-to-all(f32[16,1,1152]{2,1,0:T(1,128)S(1)} %broadcast_in_dim.27), channel_id=1, replica_groups=mesh['y'=8,'x'=4,'z'=8,'core'=2] {'z','core'}, dimensions={0} | all-to-all | bytes 147456 | tf_op jit(solution)/shard_map/all_to_all | solution.py:25
  22.7 0.2 convolution_convert_fusion.3
  23.0 0.6 fusion.44
  23.7 18.2 %all_to_all.52 = f32[32,1,320]{2,1,0:T(1,128)S(1)} all-to-all(f32[32,1,320]{2,1,0:T(1,128)S(1)} %broadcast_in_dim.29), channel_id=1, replica_groups=mesh['y'=8,'x'=4,'z'=8,'core'=2] {'y','x'}, dimensions={0} | all-to-all | bytes 81920 | tf_op jit(solution)/shard_map/all_to_all | solution.py:25
  42.3 3.4 %collective-permute-start = (bf16[8,64,256]{2,1,0:T(8,128)(2,1)S(1)}, bf16[8,64,256]{2,1,0:T(8,128)(2,1)S(1)}, u32[]{:S(2)}, u32[]{:S(2)}) collective-permute-start(bf16[8,64,256]{2,1,0:T(8,128)(2,1)S(1)} %fusion.12), channel_id=1, source_target_pairs={{0,1},{1,0},{2,3},{3,2},{4,5},{5,4},{6,7},{7,6},{8,9},{9,8},{10,11... | collective-permute-start | bytes 786440 | tf_op jit(solution)/shard_map/ppermute | solution.py:130
  45.6 1.1 collective-permute-done
  46.9 14.7 %all_to_all.53 = bf16[8,64,256]{2,1,0:T(8,128)(2,1)S(1)} all-to-all(bf16[8,64,256]{2,1,0:T(8,128)(2,1)S(1)} %add_convert_fusion), channel_id=1, replica_groups=mesh['y'=8,'x'=4,'z'=8,'core'=2] {'z'}, dimensions={0} | all-to-all | bytes 524288 | tf_op jit(solution)/shard_map/all_to_all | solution.py:25
  61.8 0.4 copy-done.3
  62.3 14.2 %all_to_all.54 = bf16[8,64,256]{2,1,0:T(8,128)(2,1)S(1)} all-to-all(bf16[8,64,256]{2,1,0:T(8,128)(2,1)S(1)} %broadcast_in_dim.31), channel_id=1, replica_groups=mesh['y'=8,'x'=4,'z'=8,'core'=2] {'z'}, dimensions={0} | all-to-all | bytes 524288 | tf_op jit(solution)/shard_map/all_to_all | solution.py:25
  76.5 2.8 %all_gather.6 = bf16[1024,256]{1,0:T(8,128)(2,1)S(1)} all-gather(bf16[512,256]{1,0:T(8,128)(2,1)S(1)} %bitcast.68), channel_id=1, replica_groups=mesh['y'=8,'x'=4,'z'=8,'core'=2] {'core'}, dimensions={0}, use_global_device_ids=true | all-gather | bytes 786432 | tf_op jit(solution)/shard_map/all_gather | solution.py:33
  79.3 0.2 convolution_convert_fusion.1
  79.6 15.5 %all_to_all.55 = bf16[8,160,128]{2,1,0:T(8,128)(2,1)S(1)} all-to-all(bf16[8,160,128]{2,1,0:T(8,128)(2,1)S(1)} %broadcast_in_dim.32), channel_id=1, replica_groups=mesh['y'=8,'x'=4,'z'=8,'core'=2] {'y'}, dimensions={0} | all-to-all | bytes 655360 | tf_op jit(solution)/shard_map/all_to_all | solution.py:25
  95.2 7.4 %all_to_all.56 = bf16[4,160,128]{2,1,0:T(8,128)(2,1)S(1)} all-to-all(bf16[4,160,128]{2,1,0:T(8,128)(2,1)S(1)} %broadcast_in_dim.34), channel_id=1, replica_groups=mesh['y'=8,'x'=4,'z'=8,'core'=2] {'x'}, dimensions={0} | all-to-all | bytes 327680 | tf_op jit(solution)/shard_map/all_to_all | solution.py:25
  102.8 0.3 fusion.7
  103.4 0.2 fusion.45
  103.7 12.6 %all_to_all.57 = f32[16,1,1024]{2,1,0:T(1,128)S(1)} all-to-all(f32[16,1,1024]{2,1,0:T(1,128)S(1)} %broadcast_in_dim.35), channel_id=1, replica_groups=mesh['y'=8,'x'=4,'z'=8,'core'=2] {'z','core'}, dimensions={0} | all-to-all | bytes 131072 | tf_op jit(solution)/shard_map/all_to_all | solution.py:25
  116.3 0.2 convolution_convert_fusion
  116.8 16.2 %all_to_all.58 = bf16[8,160,128]{2,1,0:T(8,128)(2,1)S(1)} all-to-all(bf16[8,160,128]{2,1,0:T(8,128)(2,1)S(1)} %broadcast_in_dim.36), channel_id=1, replica_groups=mesh['y'=8,'x'=4,'z'=8,'core'=2] {'y'}, dimensions={0} | all-to-all | bytes 655360 | tf_op jit(solution)/shard_map/all_to_all | solution.py:25
  133.1 7.4 %all_to_all.59 = bf16[4,160,128]{2,1,0:T(8,128)(2,1)S(1)} all-to-all(bf16[4,160,128]{2,1,0:T(8,128)(2,1)S(1)} %broadcast_in_dim.38), channel_id=1, replica_groups=mesh['y'=8,'x'=4,'z'=8,'core'=2] {'x'}, dimensions={0} | all-to-all | bytes 327680 | tf_op jit(solution)/shard_map/all_to_all | solution.py:25
  141.1 18.2 %all_gather.7 = bf16[1024,384]{1,0:T(8,128)(2,1)S(1)} all-gather(bf16[64,384]{1,0:T(8,128)(2,1)S(1)} %pad_maximum_fusion.3), channel_id=1, replica_groups=mesh['y'=8,'x'=4,'z'=8,'core'=2] {'z','core'}, dimensions={0}, use_global_device_ids=true | all-gather | bytes 835584 | tf_op jit(solution)/shard_map/all_gather | solution.py:33
  159.4 0.3 fusion.3
  159.7 0.3 fusion.46
  160.1 0.8 broadcast_divide_fusion
  (77 shorter events, 3.3 us)
Async XLA Ops:
  0.6 22.4 %copy-start = (bf16[256,256]{1,0:T(8,128)(2,1)S(1)}, bf16[256,256]{1,0:T(8,128)(2,1)}, u32[]{:S(2)}) copy-start(bf16[256,256]{1,0:T(8,128)(2,1)} %param.7) | copy-start | bytes 393220
  0.7 1.5 copy-start.4
  0.7 1.5 copy-start.5
  2.2 20.9 %copy-start.2 = (s32[1024,256]{1,0:T(8,128)S(1)}, s32[1024,256]{1,0:T(8,128)}, u32[]{:S(2)}) copy-start(s32[1024,256]{1,0:T(8,128)} %param.4) | copy-start | bytes 3145732
  42.3 4.5 %collective-permute-start = (bf16[8,64,256]{2,1,0:T(8,128)(2,1)S(1)}, bf16[8,64,256]{2,1,0:T(8,128)(2,1)S(1)}, u32[]{:S(2)}, u32[]{:S(2)}) collective-permute-start(bf16[8,64,256]{2,1,0:T(8,128)(2,1)S(1)} %fusion.12), channel_id=1, source_target_pairs={{0,1},{1,0},{2,3},{3,2},{4,5},{5,4},{6,7},{7,6},{8,9},{9,8},{10,11... | collective-permute-start | bytes 786440 | tf_op jit(solution)/shard_map/ppermute | solution.py:130
  61.6 0.6 copy-start.3
  159.3 0.8 copy-start.1
where the time goes:
time: 161 us
  blocking collectives  147 us (91%)
  matrix products  4.25 us (3%)
  starting transfers between devices  3.36 us (2%)
  other arithmetic  2.81 us (2%)
    all_to_all x9, blocking collectives, exchange(): return lax.all_to_all(blocks, axis, 0, 0, tiled=False)  126 us
    all_gather x2, blocking collectives, gather(): return lax.all_gather(block, axis, tiled=True)  21 us
    ppermute x1, starting transfers between devices, per_device(): taken = lax.ppermute(given, CORE_AXIS, [(0, 1), (1, 0)])  3.36 us
  transfers between devices with their start and end apart: 1, of which 1 were waited for; matrix products, arithmetic and copies ran while one was open for 0% of the time, Pallas kernels for 0%

commit v1 on v0

--- a/solution.py
+++ b/solution.py
@@ -21,6 +21,11 @@
 together = lax.optimization_barrier
 
 
+def all_by_exchange(x, name, d):
+    outgoing = jnp.stack([x] * lax.axis_size(name))
+    return jnp.concatenate(lax.all_to_all(outgoing, name, 0, 0), axis=d)
+
+
 def exchange(blocks, axis):
     return lax.all_to_all(blocks, axis, 0, 0, tiled=False)
 
@@ -30,7 +35,7 @@
 
 
 def gather(block, axis):
-    return lax.all_gather(block, axis, tiled=True)
+    return all_by_exchange(block, axis, 0)
 
 
 def dot(left, right):

time: 161 us -> 173 us (1.075)
  blocking collectives: 147 us -> 158 us
    all_to_all x0 -> x2, blocking collectives: none -> 32 us  [all_by_exchange(): return jnp.concatenate(lax.all_to_all(outgoing, name, 0, 0), axis=d)]
    all_gather x2 -> x0, blocking collectives: 21 us -> none  [gather(): return lax.all_gather(block, axis, tiled=True)]
where the time goes in v1:
time: 173 us; the launch traced here: 172 us
  blocking collectives  158 us (91%)
  matrix products  4.24 us (2%)
  starting transfers between devices  3.36 us (2%)
  other arithmetic  2.84 us (2%)
    all_to_all x9, blocking collectives, exchange(): return lax.all_to_all(blocks, axis, 0, 0, tiled=False)  126 us
    all_to_all x2, blocking collectives, all_by_exchange(): return jnp.concatenate(lax.all_to_all(outgoing, name, 0, 0), axis=d)  32 us
  transfers between devices with their start and end apart: 1, of which 1 were waited for; matrix products, arithmetic and copies ran while one was open for 0% of the time, Pallas kernels for 0%

profile of v1, /device:TPU:1, one launch (start us, length us, event | category | flops | bytes accessed | tf_op | source)
XLA Modules:
  0.0 172.0 jit_solution(18075572214896548566)
XLA Ops:
  0.7 1.5 fusion.9
  2.5 19.7 %all_to_all.61 = f32[16,1,1152]{2,1,0:T(1,128)S(1)} all-to-all(f32[16,1,1152]{2,1,0:T(1,128)S(1)} %broadcast_in_dim.27), channel_id=1, replica_groups=mesh['y'=8,'x'=4,'z'=8,'core'=2] {'z','core'}, dimensions={0} | all-to-all | bytes 147456 | tf_op jit(solution)/shard_map/all_to_all | solution.py:30
  22.7 0.2 convolution_convert_fusion.3
  23.0 0.6 fusion.44
  23.7 18.2 %all_to_all.62 = f32[32,1,320]{2,1,0:T(1,128)S(1)} all-to-all(f32[32,1,320]{2,1,0:T(1,128)S(1)} %broadcast_in_dim.29), channel_id=1, replica_groups=mesh['y'=8,'x'=4,'z'=8,'core'=2] {'y','x'}, dimensions={0} | all-to-all | bytes 81920 | tf_op jit(solution)/shard_map/all_to_all | solution.py:30
  42.3 3.4 %collective-permute-start = (bf16[8,64,256]{2,1,0:T(8,128)(2,1)S(1)}, bf16[8,64,256]{2,1,0:T(8,128)(2,1)S(1)}, u32[]{:S(2)}, u32[]{:S(2)}) collective-permute-start(bf16[8,64,256]{2,1,0:T(8,128)(2,1)S(1)} %fusion.12), channel_id=1, source_target_pairs={{0,1},{1,0},{2,3},{3,2},{4,5},{5,4},{6,7},{7,6},{8,9},{9,8},{10,11... | collective-permute-start | bytes 786440 | tf_op jit(solution)/shard_map/ppermute | solution.py:135
  45.6 1.1 collective-permute-done
  46.9 14.7 %all_to_all.63 = bf16[8,64,256]{2,1,0:T(8,128)(2,1)S(1)} all-to-all(bf16[8,64,256]{2,1,0:T(8,128)(2,1)S(1)} %add_convert_fusion), channel_id=1, replica_groups=mesh['y'=8,'x'=4,'z'=8,'core'=2] {'z'}, dimensions={0} | all-to-all | bytes 524288 | tf_op jit(solution)/shard_map/all_to_all | solution.py:30
  61.8 0.4 copy-done.3
  62.3 14.2 %all_to_all.64 = bf16[8,64,256]{2,1,0:T(8,128)(2,1)S(1)} all-to-all(bf16[8,64,256]{2,1,0:T(8,128)(2,1)S(1)} %broadcast_in_dim.31), channel_id=1, replica_groups=mesh['y'=8,'x'=4,'z'=8,'core'=2] {'z'}, dimensions={0} | all-to-all | bytes 524288 | tf_op jit(solution)/shard_map/all_to_all | solution.py:30
  76.5 4.8 %all_to_all.65 = bf16[2,512,256]{2,1,0:T(8,128)(2,1)S(1)} all-to-all(bf16[2,512,256]{2,1,0:T(8,128)(2,1)S(1)} %pad_maximum_fusion), channel_id=1, replica_groups=mesh['y'=8,'x'=4,'z'=8,'core'=2] {'core'}, dimensions={0} | all-to-all | bytes 1048576 | tf_op jit(solution)/shard_map/all_to_all | solution.py:26
  81.3 0.2 convolution_convert_fusion.1
  81.6 15.5 %all_to_all.66 = bf16[8,160,128]{2,1,0:T(8,128)(2,1)S(1)} all-to-all(bf16[8,160,128]{2,1,0:T(8,128)(2,1)S(1)} %broadcast_in_dim.32), channel_id=1, replica_groups=mesh['y'=8,'x'=4,'z'=8,'core'=2] {'y'}, dimensions={0} | all-to-all | bytes 655360 | tf_op jit(solution)/shard_map/all_to_all | solution.py:30
  97.2 7.4 %all_to_all.67 = bf16[4,160,128]{2,1,0:T(8,128)(2,1)S(1)} all-to-all(bf16[4,160,128]{2,1,0:T(8,128)(2,1)S(1)} %broadcast_in_dim.34), channel_id=1, replica_groups=mesh['y'=8,'x'=4,'z'=8,'core'=2] {'x'}, dimensions={0} | all-to-all | bytes 327680 | tf_op jit(solution)/shard_map/all_to_all | solution.py:30
  104.9 0.3 fusion.7
  105.4 0.2 fusion.45
  105.7 12.6 %all_to_all.68 = f32[16,1,1024]{2,1,0:T(1,128)S(1)} all-to-all(f32[16,1,1024]{2,1,0:T(1,128)S(1)} %broadcast_in_dim.35), channel_id=1, replica_groups=mesh['y'=8,'x'=4,'z'=8,'core'=2] {'z','core'}, dimensions={0} | all-to-all | bytes 131072 | tf_op jit(solution)/shard_map/all_to_all | solution.py:30
  118.3 0.2 convolution_convert_fusion
  118.9 16.2 %all_to_all.69 = bf16[8,160,128]{2,1,0:T(8,128)(2,1)S(1)} all-to-all(bf16[8,160,128]{2,1,0:T(8,128)(2,1)S(1)} %broadcast_in_dim.36), channel_id=1, replica_groups=mesh['y'=8,'x'=4,'z'=8,'core'=2] {'y'}, dimensions={0} | all-to-all | bytes 655360 | tf_op jit(solution)/shard_map/all_to_all | solution.py:30
  135.1 7.4 %all_to_all.70 = bf16[4,160,128]{2,1,0:T(8,128)(2,1)S(1)} all-to-all(bf16[4,160,128]{2,1,0:T(8,128)(2,1)S(1)} %broadcast_in_dim.38), channel_id=1, replica_groups=mesh['y'=8,'x'=4,'z'=8,'core'=2] {'x'}, dimensions={0} | all-to-all | bytes 327680 | tf_op jit(solution)/shard_map/all_to_all | solution.py:30
  143.2 27.2 %all_to_all.71 = bf16[16,64,384]{2,1,0:T(8,128)(2,1)S(1)} all-to-all(bf16[16,64,384]{2,1,0:T(8,128)(2,1)S(1)} %stack.5), channel_id=1, replica_groups=mesh['y'=8,'x'=4,'z'=8,'core'=2] {'z','core'}, dimensions={0} | all-to-all | bytes 1572864 | tf_op jit(solution)/shard_map/all_to_all | solution.py:26
  170.4 0.3 fusion.3
  170.7 0.3 fusion.46
  171.2 0.8 broadcast_divide_fusion
  (79 shorter events, 3.5 us)
Async XLA Ops:
  0.6 22.4 %copy-start = (bf16[256,256]{1,0:T(8,128)(2,1)S(1)}, bf16[256,256]{1,0:T(8,128)(2,1)}, u32[]{:S(2)}) copy-start(bf16[256,256]{1,0:T(8,128)(2,1)} %param.7) | copy-start | bytes 393220
  0.7 1.5 copy-start.4
  0.7 1.5 copy-start.5
  2.2 20.9 %copy-start.2 = (s32[1024,256]{1,0:T(8,128)S(1)}, s32[1024,256]{1,0:T(8,128)}, u32[]{:S(2)}) copy-start(s32[1024,256]{1,0:T(8,128)} %param.4) | copy-start | bytes 3145732
  42.3 4.5 %collective-permute-start = (bf16[8,64,256]{2,1,0:T(8,128)(2,1)S(1)}, bf16[8,64,256]{2,1,0:T(8,128)(2,1)S(1)}, u32[]{:S(2)}, u32[]{:S(2)}) collective-permute-start(bf16[8,64,256]{2,1,0:T(8,128)(2,1)S(1)} %fusion.12), channel_id=1, source_target_pairs={{0,1},{1,0},{2,3},{3,2},{4,5},{5,4},{6,7},{7,6},{8,9},{9,8},{10,11... | collective-permute-start | bytes 786440 | tf_op jit(solution)/shard_map/ppermute | solution.py:135
  61.6 0.6 copy-start.3
  170.4 0.8 copy-start.1
